TPU v7x, 32 devices: a whole 2x2x4 slice. The times are simulated.
32 devices in a mesh: facet: 4 (over z), col: 8 (over y, x, core).
Axes of the slice: x: 2, y: 2, z: 4, core: 2. Of those that a mesh axis runs over, the one named last changes fastest.
Arguments:
- facets: bfloat16 [4, 64, 2, 128], P('facet', 'col'), may hold values from -6 to 6
- sub_offsets: int32 [8, 4], P('col'), may hold values from 0 to 8191
- col_offsets: int32 [8], P('col'), may hold values from 0 to 8191
- screen_index: int32 [8, 4], P('col', 'facet'), may hold values from 0 to 3
- screens: float32 [4, 2, 256, 256], replicated, may hold values from -6 to 6
Outputs:
- facets_out: float32 [4, 64, 2, 128], P('facet', 'col')
All inputs are finite; a program needn't handle non-finite values.
Results may differ from a plain program's by a relative error of at most 0.0056.
Values may be sent and summed in bfloat16 or wider, within the bound.
No kernel may reach another device: no remote copies, remote signals or barrier semaphores. Data moves between devices by JAX's collectives and lax.ppermute only.
A program may use at most 64 MiB of HBM per device.

v0:
```python
import math
import jax
import jax.numpy as jnp
from jax import lax
from jax.sharding import PartitionSpec as P

XC = 64
XS = 256
SLAB = 128
NPAD = 8192


def phase_pair(numerator, period, direction, factor):
    angles = direction * 2.0 * math.pi / period * numerator.astype(jnp.float32)
    return (
        (jnp.cos(angles) * factor).astype(jnp.bfloat16),
        (jnp.sin(angles) * factor).astype(jnp.bfloat16),
    )


def embed_table(facet_ids):
    column = jnp.arange(XS, dtype=jnp.int32)
    within = jnp.arange(XC, dtype=jnp.int32)
    product = column[None, :, None] * (within[None, None, :] + 7 * facet_ids[:, None, None]) % XS
    return phase_pair(product, XS, 1.0, 1.0 / math.sqrt(XS))


def column_table(offset):
    position = jnp.arange(SLAB, dtype=jnp.int32)
    frequency = (offset + jnp.arange(XC, dtype=jnp.int32)) % NPAD
    product = position[:, None] * frequency[None, :] % NPAD
    return phase_pair(product, NPAD, -1.0, 1.0 / math.sqrt(SLAB))


def row_table(offsets, row_ids, height):
    frequency = (offsets[:, None] + jnp.arange(XC, dtype=jnp.int32)[None, :]) % NPAD
    frequency = frequency.reshape(frequency.shape + (1,) * row_ids.ndim)
    product = frequency * (row_ids % NPAD) % NPAD
    return phase_pair(product, NPAD, -1.0, 1.0 / math.sqrt(height))


def general_dot(first_op, second_op, contract):
    numbers = ((contract[0], contract[1]), ((), ()))
    return lax.dot_general(first_op, second_op, numbers, preferred_element_type=jnp.float32)


def complex_dot(first_op, second_op, contract):
    real_part = general_dot(first_op[0], second_op[0], contract) - general_dot(
        first_op[1], second_op[1], contract
    )
    imag_part = general_dot(first_op[0], second_op[1], contract) + general_dot(
        first_op[1], second_op[0], contract
    )
    return (real_part, imag_part)


def complex_einsum(form, first_op, second_op):

    def single(left_part, right_part):
        return jnp.einsum(form, left_part, right_part, preferred_element_type=jnp.float32)

    real_part = single(first_op[0], second_op[0]) - single(first_op[1], second_op[1])
    imag_part = single(first_op[0], second_op[1]) + single(first_op[1], second_op[0])
    return (real_part, imag_part)


def round_pair(values):
    return (values[0].astype(jnp.bfloat16), values[1].astype(jnp.bfloat16))


def body(facets, sub_offsets, col_offsets, screen_index, screens):
    facet_now = lax.axis_index("facet")
    facet_count = lax.axis_size("facet")
    column_count = lax.axis_size("col")
    local_rows = facets.shape[1]
    total_rows = local_rows * column_count
    subgrid_count = sub_offsets.shape[1]
    across = column_table(col_offsets[0])
    row_ids = facet_now * total_rows + jnp.arange(total_rows, dtype=jnp.int32)
    row_phase = row_table(sub_offsets[0], row_ids, total_rows)
    row_flat = (
        row_phase[0].reshape(subgrid_count * XC, total_rows),
        row_phase[1].reshape(subgrid_count * XC, total_rows),
    )
    embedding = embed_table(jnp.arange(facet_count, dtype=jnp.int32))
    adjoint_embed = (embedding[0], -embedding[1])
    whole_slab = lax.all_gather(facets[0], "col", axis=0, tiled=True)
    spread = round_pair(complex_dot((whole_slab[:, 0], whole_slab[:, 1]), across, ((1,), (0,))))
    block_phase = (row_flat[0], row_flat[1])
    summand = complex_dot(block_phase, spread, ((1,), (0,)))
    contrib_real = summand[0]
    contrib_imag = summand[1]
    contributions = jnp.stack(
        [contrib_real.reshape(subgrid_count, XC, XC), contrib_imag.reshape(subgrid_count, XC, XC)],
        axis=1,
    ).astype(jnp.bfloat16)
    outgoing = contributions.reshape(facet_count, subgrid_count // facet_count, 2, XC, XC)
    received = lax.all_to_all(outgoing, "facet", split_axis=0, concat_axis=0, tiled=True)
    factor = 1.0 / math.sqrt(received.shape[0])
    halfway = round_pair(
        complex_einsum("fkuv,fav->fkua", (received[:, :, 0], received[:, :, 1]), embedding)
    )
    subgrid = complex_einsum("fau,fkub->kab", embedding, halfway)
    subgrids = jnp.stack([subgrid[0] * factor, subgrid[1] * factor], axis=1)
    gain_maps = jnp.take(screens, screen_index[0], axis=0)
    sub_real = subgrids[:, 0]
    sub_imag = subgrids[:, 1]
    gain_real = gain_maps[:, 0]
    gain_imag = gain_maps[:, 1]
    screened = jnp.stack(
        [sub_real * gain_real - sub_imag * gain_imag, sub_real * gain_imag + sub_imag * gain_real],
        axis=1,
    ).astype(jnp.bfloat16)
    inner = round_pair(
        complex_einsum("fau,kab->fkub", adjoint_embed, (screened[:, 0], screened[:, 1]))
    )
    returned = round_pair(complex_einsum("fkub,fbv->fkuv", inner, adjoint_embed))
    going_back = jnp.stack([returned[0], returned[1]], axis=2)
    arrived = lax.all_to_all(going_back, "facet", split_axis=0, concat_axis=0, tiled=True)
    flat_parts = (
        arrived[:, :, 0].reshape(subgrid_count * XC, XC),
        arrived[:, :, 1].reshape(subgrid_count * XC, XC),
    )
    conj_rows = (row_flat[0], -row_flat[1])
    conj_across = (across[0], -across[1])
    block_phase = (conj_rows[0], conj_rows[1])
    slab_rows = round_pair(complex_dot(block_phase, flat_parts, ((0,), (0,))))
    summand = complex_dot(slab_rows, conj_across, ((1,), (1,)))
    summed = lax.psum_scatter(
        jnp.stack([summand[0], summand[1]], axis=1), "col", scatter_dimension=0, tiled=True
    )
    factor = 1.0 / math.sqrt(column_count * subgrid_count)
    return (summed * factor)[None]


def solution(mesh):
    return jax.shard_map(
        body,
        mesh=mesh,
        in_specs=(P("facet", "col", None, None), P("col", None), P("col"), P("col", "facet"), P()),
        out_specs=P("facet", "col", None, None),
        check_vma=False,
    )
```

profile of v0, /device:TPU:0, one launch (start us, length us, event | category | flops | bytes accessed | tf_op | source)
XLA Modules:
  0.0 103.0 jit_solution(15256467704068832730)
XLA Ops:
  6.5 0.0 copy-start
  7.4 0.7 copy.23
  8.0 10.3 %all-gather = bf16[1,64,2,128]{3,1,2,0:T(8,128)(2,1)S(1)} all-gather(bf16[1,8,2,128]{3,1,2,0:T(8,128)(2,1)S(1)} %copy.23), channel_id=2, replica_groups=mesh['facet'=4,'col'=8] {'col'}, dimensions={1}, use_global_device_ids=true | all-gather | bytes 36864 | tf_op jit(solution)/shard_map/all_gather | solution.py:87
  18.4 0.4 fusion.56
  18.8 0.4 fusion.54
  19.2 0.4 fusion.17
  19.7 0.7 iota_add_fusion.1
  20.4 0.1 add.272
  20.5 0.4 fusion.16
  20.9 0.7 fusion.47
  21.6 0.7 fusion.48
  22.3 0.7 fusion.13
  23.0 0.1 copy.40
  23.1 0.7 fusion.12
  23.8 0.1 copy.39
  24.0 0.8 reshape.305
  24.8 4.9 %all-to-all-start = ((bf16[4,2,4096]{2,1,0:T(2,128)(2,1)}), bf16[4,2,4096]{2,1,0:T(2,128)(2,1)S(1)}, u32[]{:S(2)}, u32[]{:S(2)}) async-start(bf16[4,2,4096]{2,1,0:T(2,128)(2,1)} %reshape.305), calls=%async_computation | async-start | bytes 131072 | tf_op jit(solution)/shard_map/all_to_all | solution.py:98
  29.6 0.0 reduce-scatter.2.cloned.1.call-start
  30.3 0.0 copy-done
  30.4 0.2 copy.43
  30.6 0.1 iota_add_fusion
  30.7 1.1 %multiply_convert_fusion.1 = bf16[4,256,64]{1,2,0:T(8,128)(2,1)S(1)} fusion(s32[4,64]{1,0:T(4,128)S(1)} %iota_add_fusion), kind=kLoop, calls=%fused_computation.50 | loop fusion | flops 1048576 | bytes 132096 | tf_op jit(solution)/shard_map/convert_element_type | solution.py:16
  31.8 1.1 %fusion.33 = bf16[4,256,64]{1,2,0:T(8,128)(2,1)S(1)} fusion(s32[4,64]{1,0:T(4,128)S(1)} %iota_add_fusion), kind=kLoop, calls=%fused_computation.68 | loop fusion | flops 1245184 | bytes 132096 | tf_op jit(solution)/shard_map/neg | solution.py:86
  32.8 2.5 %all-to-all-done = bf16[4,2,4096]{2,1,0:T(2,128)(2,1)S(1)} async-done(((bf16[4,2,4096]{2,1,0:T(2,128)(2,1)}), bf16[4,2,4096]{2,1,0:T(2,128)(2,1)S(1)}, u32[]{:S(2)}, u32[]{:S(2)}) %all-to-all-start) | async-done | bytes 65568 | tf_op jit(solution)/shard_map/all_to_all | solution.py:98
  35.4 0.1 reshape.306
  35.5 1.6 %fusion.34 = f32[4,64,256]{2,1,0:T(8,128)S(1)} fusion(s32[4,64]{1,0:T(4,128)S(1)} %iota_add_fusion, bf16[4,1,2,64,64]{4,3,2,1,0:T(8,128)(2,1)S(1)} %reshape.306), kind=kOutput, calls=%fused_computation.69 | convolution fusion | flops 9437184 | bytes 329728 | tf_op jit(solution)/shard_map/fkuv,fav->fkua/dot_general | solution.py:60
  37.2 1.4 %fusion.36 = f32[4,64,256]{2,1,0:T(8,128)S(1)} fusion(s32[4,64]{1,0:T(4,128)S(1)} %iota_add_fusion, bf16[4,1,2,64,64]{4,3,2,1,0:T(8,128)(2,1)S(1)} %reshape.306), kind=kOutput, calls=%fused_computation.71 | convolution fusion | flops 9437184 | bytes 329728 | tf_op jit(solution)/shard_map/fkuv,fav->fkua/dot_general | solution.py:60
  38.6 1.2 %fusion.7 = bf16[4,64,256]{2,1,0:T(8,128)(2,1)S(1)} fusion(f32[4,64,256]{2,1,0:T(8,128)S(1)} %fusion.34, s32[4,64]{1,0:T(4,128)S(1)} %iota_add_fusion, bf16[4,1,2,64,64]{4,3,2,1,0:T(8,128)(2,1)S(1)} %reshape.306), kind=kOutput, calls=%fused_computation.13 | convolution fusion | flops 9568256 | bytes 460800 | tf_op jit(solution)/shard_map/fkuv,fav->fkua/dot_general | solution.py:60
  39.8 1.2 %convolution_bitcast_fusion.2 = f32[256,256]{1,0:T(8,128)S(1)} fusion(bf16[4,64,256]{2,1,0:T(8,128)(2,1)S(1)} %fusion.7, s32[4,64]{1,0:T(4,128)S(1)} %iota_add_fusion), kind=kOutput, calls=%fused_computation.4 | convolution fusion | flops 34603008 | bytes 394240 | tf_op jit(solution)/shard_map/fau,fkub->kab/dot_general | solution.py:60
  41.0 1.2 %fusion.6 = bf16[4,64,256]{2,1,0:T(8,128)(2,1)S(1)} fusion(f32[4,64,256]{2,1,0:T(8,128)S(1)} %fusion.36, s32[4,64]{1,0:T(4,128)S(1)} %iota_add_fusion, bf16[4,1,2,64,64]{4,3,2,1,0:T(8,128)(2,1)S(1)} %reshape.306), kind=kOutput, calls=%fused_computation.12 | convolution fusion | flops 9568256 | bytes 460800 | tf_op jit(solution)/shard_map/fkuv,fav->fkua/dot_general | solution.py:60
  42.2 1.2 %convolution_bitcast_fusion = f32[256,256]{1,0:T(8,128)S(1)} fusion(bf16[4,64,256]{2,1,0:T(8,128)(2,1)S(1)} %fusion.6, s32[4,64]{1,0:T(4,128)S(1)} %iota_add_fusion), kind=kOutput, calls=%fused_computation.2 | convolution fusion | flops 34603008 | bytes 394240 | tf_op jit(solution)/shard_map/fau,fkub->kab/dot_general | solution.py:60
  43.4 1.2 %fusion.2 = f32[1,256,256]{1,2,0:T(8,128)S(1)} fusion(f32[256,256]{1,0:T(8,128)S(1)} %convolution_bitcast_fusion.2, bf16[4,64,256]{2,1,0:T(8,128)(2,1)S(1)} %fusion.6, s32[4,64]{1,0:T(4,128)S(1)} %iota_add_fusion), kind=kOutput, calls=%fused_computation.8 | convolution fusion | flops 34734080 | bytes 656384 | tf_op jit(solution)/shard_map/fau,fkub->kab/dot_general | solution.py:60
  44.6 1.2 %fusion.30 = (bf16[256,256]{0,1:T(8,128)(2,1)S(1)}, bf16[256,256]{0,1:T(8,128)(2,1)S(1)}) fusion(f32[1,2,256,256]{2,3,1,0:T(8,128)S(1)} %broadcast_select_fusion, f32[1,256,256]{1,2,0:T(8,128)S(1)} %fusion.2, f32[256,256]{1,0:T(8,128)S(1)} %convolution_bitcast_fusion, bf16[4,64,256]{2,1,0:T(8,128)(2,1)S(1)} %fusion.7, s32[4,64]{1,0:T(4,128)S(1)} %iota_add_fusion), kind=kOutput, calls=%fused_computation.63 | convolution fusion | flops 35258368 | bytes 1442816 | tf_op jit(solution)/shard_map/fau,fkub->kab/dot_general | solution.py:60
  45.8 0.2 fusion.204
  46.1 0.2 fusion.206
  46.3 0.2 fusion.205
  46.5 0.2 fusion.207
  46.8 1.4 %fusion.38 = f32[4,64,64]{2,1,0:T(8,128)S(1)} fusion(bf16[4,64,256]{2,1,0:T(8,128)(2,1)S(1)} %fusion.31, s32[4,64]{1,0:T(4,128)S(1)} %iota_add_fusion), kind=kOutput, calls=%fused_computation.77 | convolution fusion | flops 9633792 | bytes 197632 | tf_op jit(solution)/shard_map/fkub,fbv->fkuv/dot_general | solution.py:60
  48.2 1.4 %fusion.35 = f32[4,64,64]{2,1,0:T(8,128)S(1)} fusion(bf16[4,64,256]{2,1,0:T(8,128)(2,1)S(1)} %fusion.31, s32[4,64]{1,0:T(4,128)S(1)} %iota_add_fusion), kind=kOutput, calls=%fused_computation.70 | convolution fusion | flops 9437184 | bytes 197632 | tf_op jit(solution)/shard_map/fkub,fbv->fkuv/dot_general | solution.py:60
  49.6 0.1 fusion.32
  49.7 1.2 %fusion.10 = bf16[4,1,1,64,64]{4,3,0,2,1:T(8,128)(2,1)S(1)} fusion(f32[4,64,64]{2,1,0:T(8,128)S(1)} %fusion.38, bf16[4,64,256]{2,1,0:T(8,128)(2,1)S(1)} %fusion.32, s32[4,64]{1,0:T(4,128)S(1)} %iota_add_fusion), kind=kOutput, calls=%fused_computation.20 | convolution fusion | flops 9469952 | bytes 230400 | tf_op jit(solution)/shard_map/fkub,fbv->fkuv/dot_general | solution.py:60
  50.9 1.2 %fusion.11 = bf16[4,1,1,64,64]{4,3,0,2,1:T(8,128)(2,1)S(1)} fusion(f32[4,64,64]{2,1,0:T(8,128)S(1)} %fusion.35, bf16[4,64,256]{2,1,0:T(8,128)(2,1)S(1)} %fusion.32, s32[4,64]{1,0:T(4,128)S(1)} %iota_add_fusion), kind=kOutput, calls=%fused_computation.21 | convolution fusion | flops 9666560 | bytes 230400 | tf_op jit(solution)/shard_map/fkub,fbv->fkuv/dot_general | solution.py:60
  52.1 0.2 reshape.307
  52.3 8.1 %all_to_all.10 = bf16[4,2,4096]{2,1,0:T(2,128)(2,1)S(1)} all-to-all(bf16[4,2,4096]{2,1,0:T(2,128)(2,1)S(1)} %reshape.307), channel_id=1, replica_groups=mesh['facet'=4,'col'=8] {'facet'}, dimensions={0} | all-to-all | bytes 131072 | tf_op jit(solution)/shard_map/all_to_all | solution.py:119
  60.4 0.1 reshape.308
  60.5 0.7 fusion.46
  61.3 0.7 fusion.45
  62.0 0.7 fusion.18
  62.7 0.4 fusion.57
  63.1 0.4 fusion.53
  63.5 0.7 fusion.19
  64.3 0.4 fusion.14
  64.6 0.4 fusion.15
  65.0 0.6 pad_maximum_fusion.2
  65.7 0.0 reduce-scatter.2.cloned.1.call-update
  65.7 29.2 %reduce-scatter.2.cloned.1.call-done = f32[8,2,128]{2,0,1:T(8,128)} async-done(((f32[64,2,128]{2,0,1:T(8,128)}), f32[8,2,128]{2,0,1:T(8,128)}) %reduce-scatter.2.cloned.1.call-update) | async-done | bytes 8208 | tf_op jit(solution)/shard_map/reduce_scatter | solution.py:129
  94.8 0.7 multiply_bitcast_fusion
  95.5 0.6 copy.34
  (11 shorter events, 0.2 us)
Async XLA Ops:
  6.5 23.8 %copy-start = (f32[4,2,256,256]{3,2,1,0:T(8,128)S(1)}, f32[4,2,256,256]{3,2,1,0:T(8,128)}, u32[]{:S(2)}) copy-start(f32[4,2,256,256]{3,2,1,0:T(8,128)} %param.9) | copy-start | bytes 6291460
  24.8 10.6 %all-to-all-start = ((bf16[4,2,4096]{2,1,0:T(2,128)(2,1)}), bf16[4,2,4096]{2,1,0:T(2,128)(2,1)S(1)}, u32[]{:S(2)}, u32[]{:S(2)}) async-start(bf16[4,2,4096]{2,1,0:T(2,128)(2,1)} %reshape.305), calls=%async_computation | async-start | bytes 131072 | tf_op jit(solution)/shard_map/all_to_all | solution.py:98
  29.6 65.2 %reduce-scatter.2.cloned.1.call-start = ((), (), s32[]{:S(2)}) async-start(), calls=%async_computation.3 | async-start | bytes 73728 | tf_op jit(solution)/shard_map/reduce_scatter | solution.py:129
Sparse Core Ops, SparseCore 0:
  65.8 28.9 reduce-scatter.1
where the time goes:
time: 103 us
  waiting for transfers between devices  31.7 us (31%)
  matrix products  25.2 us (24%)
  blocking collectives  18.4 us (18%)
  between operations  15.1 us (15%)
  starting transfers between devices  4.87 us (5%)
  other arithmetic  4.49 us (4%)
  local copies, waits for them, and re-layouts  3.13 us (3%)
    reduce_scatter x1, waiting for transfers between devices, body(): lax.psum_scatter(jnp.stack([summand[0], summand[1]], axis=1), 'col', scat...  29.2 us
    dot_general x12, matrix products, single(): jnp.einsum(form, left_part, right_part, preferred_element_type=jnp.float32)  15.4 us
    all_gather x1, blocking collectives, body(): whole_slab = lax.all_gather(facets[0], 'col', axis=0, tiled=True)  10.3 us
    dot_general x16, matrix products, general_dot(): lax.dot_general(first_op, second_op, numbers, preferred_element_type=jnp....  8.9 us
    all_to_all x1, blocking collectives, body(): lax.all_to_all(going_back, 'facet', split_axis=0, concat_axis=0, tiled=True)  8.11 us
    all_to_all x1, starting transfers between devices, body(): lax.all_to_all(outgoing, 'facet', split_axis=0, concat_axis=0, tiled=True)  4.87 us
    all_to_all x1, waiting for transfers between devices, body(): lax.all_to_all(outgoing, 'facet', split_axis=0, concat_axis=0, tiled=True)  2.54 us
    unnamed x8, local copies, waits for them, and re-layouts  2.12 us
  transfers between devices with their start and end apart: 2, of which 2 were waited for; matrix products, arithmetic and copies ran while one was open for 2% of the time, Pallas kernels for 0%

commit v1 on v0

--- a/solution.py
+++ b/solution.py
@@ -84,7 +84,9 @@
     )
     embedding = embed_table(jnp.arange(facet_count, dtype=jnp.int32))
     adjoint_embed = (embedding[0], -embedding[1])
-    whole_slab = lax.all_gather(facets[0], "col", axis=0, tiled=True)
+    whole_slab = jnp.concatenate(
+        lax.all_to_all(jnp.stack([facets[0]] * lax.axis_size("col")), "col", 0, 0), axis=0
+    )
     spread = round_pair(complex_dot((whole_slab[:, 0], whole_slab[:, 1]), across, ((1,), (0,))))
     block_phase = (row_flat[0], row_flat[1])
     summand = complex_dot(block_phase, spread, ((1,), (0,)))

time: 103 us -> 102 us (level)
  blocking collectives: 18.4 us -> 8.11 us
  starting transfers between devices: 4.87 us -> 10.1 us
  waiting for transfers between devices: 31.7 us -> 35.3 us
    all_gather x1 -> x0, blocking collectives: 10.3 us -> none  [body(): whole_slab = lax.all_gather(facets[0], 'col', axis=0, tiled=True)]
    all_to_all x0 -> x1, starting transfers between devices: none -> 5.2 us  [body(): lax.all_to_all(jnp.stack([facets[0]] * lax.axis_size('col')), 'col', 0, 0)]
    all_to_all x1, waiting for transfers between devices: 2.54 us -> 4.67 us  [body(): lax.all_to_all(outgoing, 'facet', split_axis=0, concat_axis=0, tiled=True)]
    all_to_all x0 -> x1, waiting for transfers between devices: none -> 1.85 us  [body(): lax.all_to_all(jnp.stack([facets[0]] * lax.axis_size('col')), 'col', 0, 0)]
    another operation x0 -> x2, local copies, waits for them, and re-layouts: none -> 1.45 us
    unnamed x8 -> x9, local copies, waits for them, and re-layouts: 2.12 us -> 1.45 us
  transfers between devices with their start and end apart: 2 -> 3, of which waited for: 2 -> 3; matrix products, arithmetic and copies ran while one was open for 2% -> 3% of each run, Pallas kernels for 0% -> 0%
where the time goes in v1:
time: 102 us; the launch traced here: 101 us
  waiting for transfers between devices  35.3 us (35%)
  matrix products  25.2 us (25%)
  between operations  15 us (15%)
  starting transfers between devices  10.1 us (10%)
  blocking collectives  8.11 us (8%)
  local copies, waits for them, and re-layouts  3.91 us (4%)
  other arithmetic  3.84 us (4%)
    reduce_scatter x1, waiting for transfers between devices, body(): lax.psum_scatter(jnp.stack([summand[0], summand[1]], axis=1), 'col', scat...  28.8 us
    dot_general x12, matrix products, single(): jnp.einsum(form, left_part, right_part, preferred_element_type=jnp.float32)  15.4 us
    dot_general x16, matrix products, general_dot(): lax.dot_general(first_op, second_op, numbers, preferred_element_type=jnp....  8.91 us
    all_to_all x1, blocking collectives, body(): lax.all_to_all(going_back, 'facet', split_axis=0, concat_axis=0, tiled=True)  8.11 us
    all_to_all x1, starting transfers between devices, body(): lax.all_to_all(jnp.stack([facets[0]] * lax.axis_size('col')), 'col', 0, 0)  5.2 us
    all_to_all x1, starting transfers between devices, body(): lax.all_to_all(outgoing, 'facet', split_axis=0, concat_axis=0, tiled=True)  4.87 us
    all_to_all x1, waiting for transfers between devices, body(): lax.all_to_all(outgoing, 'facet', split_axis=0, concat_axis=0, tiled=True)  4.67 us
  transfers between devices with their start and end apart: 3, of which 3 were waited for; matrix products, arithmetic and copies ran while one was open for 3% of the time, Pallas kernels for 0%

profile of v1, /device:TPU:0, one launch (start us, length us, event | category | flops | bytes accessed | tf_op | source)
XLA Modules:
  0.0 101.5 jit_solution(10599858393245978030)
XLA Ops:
  6.5 0.0 copy-start
  6.5 0.0 copy-start.1
  6.5 0.8 copy.23
  7.4 0.6 stack.31
  8.0 5.2 %all-to-all-start = ((bf16[8,8,2,128]{3,1,2,0:T(8,128)(2,1)}), bf16[8,8,2,128]{3,1,2,0:T(8,128)(2,1)S(1)}, u32[]{:S(2)}, u32[]{:S(2)}) async-start(bf16[8,8,2,128]{3,1,2,0:T(8,128)(2,1)} %stack.31), calls=%async_computation | async-start | bytes 65536 | tf_op jit(solution)/shard_map/all_to_all | solution.py:88
  13.9 0.0 copy-done
  13.9 0.2 copy.44
  14.1 0.1 iota_add_fusion
  14.9 0.0 copy-done.1
  14.9 0.1 iota_add_fusion.1
  14.9 0.1 add.272
  15.0 1.1 %multiply_convert_fusion.1 = bf16[4,256,64]{1,2,0:T(8,128)(2,1)S(1)} fusion(s32[4,64]{1,0:T(4,128)S(1)} %iota_add_fusion), kind=kLoop, calls=%fused_computation.50 | loop fusion | flops 1048576 | bytes 132096 | tf_op jit(solution)/shard_map/convert_element_type | solution.py:16
  16.2 1.9 %all-to-all-done = bf16[8,8,2,128]{3,1,2,0:T(8,128)(2,1)S(1)} async-done(((bf16[8,8,2,128]{3,1,2,0:T(8,128)(2,1)}), bf16[8,8,2,128]{3,1,2,0:T(8,128)(2,1)S(1)}, u32[]{:S(2)}, u32[]{:S(2)}) %all-to-all-start) | async-done | bytes 32800 | tf_op jit(solution)/shard_map/all_to_all | solution.py:88
  18.0 0.4 fusion.56
  18.5 0.4 fusion.54
  18.9 0.4 fusion.17
  19.3 0.4 fusion.16
  19.7 0.7 fusion.47
  20.4 0.7 fusion.48
  21.1 0.7 fusion.13
  21.8 0.1 copy.41
  21.9 0.7 fusion.12
  22.6 0.1 copy.40
  22.8 0.8 reshape.309
  23.6 4.9 %all-to-all-start.1 = ((bf16[4,2,4096]{2,1,0:T(2,128)(2,1)}), bf16[4,2,4096]{2,1,0:T(2,128)(2,1)S(1)}, u32[]{:S(2)}, u32[]{:S(2)}) async-start(bf16[4,2,4096]{2,1,0:T(2,128)(2,1)} %reshape.309), calls=%async_computation.1 | async-start | bytes 131072 | tf_op jit(solution)/shard_map/all_to_all | solution.py:100
  28.5 0.0 reduce-scatter.2.cloned.1.call-start
  28.5 1.1 %fusion.33 = bf16[4,256,64]{1,2,0:T(8,128)(2,1)S(1)} fusion(s32[4,64]{1,0:T(4,128)S(1)} %iota_add_fusion), kind=kLoop, calls=%fused_computation.68 | loop fusion | flops 1245184 | bytes 132096 | tf_op jit(solution)/shard_map/neg | solution.py:86
  29.6 4.7 %all-to-all-done.1 = bf16[4,2,4096]{2,1,0:T(2,128)(2,1)S(1)} async-done(((bf16[4,2,4096]{2,1,0:T(2,128)(2,1)}), bf16[4,2,4096]{2,1,0:T(2,128)(2,1)S(1)}, u32[]{:S(2)}, u32[]{:S(2)}) %all-to-all-start.1) | async-done | bytes 65568 | tf_op jit(solution)/shard_map/all_to_all | solution.py:100
  34.2 0.1 reshape.310
  34.4 1.6 %fusion.34 = f32[4,64,256]{2,1,0:T(8,128)S(1)} fusion(s32[4,64]{1,0:T(4,128)S(1)} %iota_add_fusion, bf16[4,1,2,64,64]{4,3,2,1,0:T(8,128)(2,1)S(1)} %reshape.310), kind=kOutput, calls=%fused_computation.69 | convolution fusion | flops 9437184 | bytes 329728 | tf_op jit(solution)/shard_map/fkuv,fav->fkua/dot_general | solution.py:60
  36.0 1.4 %fusion.36 = f32[4,64,256]{2,1,0:T(8,128)S(1)} fusion(s32[4,64]{1,0:T(4,128)S(1)} %iota_add_fusion, bf16[4,1,2,64,64]{4,3,2,1,0:T(8,128)(2,1)S(1)} %reshape.310), kind=kOutput, calls=%fused_computation.71 | convolution fusion | flops 9437184 | bytes 329728 | tf_op jit(solution)/shard_map/fkuv,fav->fkua/dot_general | solution.py:60
  37.4 1.2 %fusion.7 = bf16[4,64,256]{2,1,0:T(8,128)(2,1)S(1)} fusion(f32[4,64,256]{2,1,0:T(8,128)S(1)} %fusion.34, s32[4,64]{1,0:T(4,128)S(1)} %iota_add_fusion, bf16[4,1,2,64,64]{4,3,2,1,0:T(8,128)(2,1)S(1)} %reshape.310), kind=kOutput, calls=%fused_computation.13 | convolution fusion | flops 9568256 | bytes 460800 | tf_op jit(solution)/shard_map/fkuv,fav->fkua/dot_general | solution.py:60
  38.6 1.2 %convolution_bitcast_fusion.2 = f32[256,256]{1,0:T(8,128)S(1)} fusion(bf16[4,64,256]{2,1,0:T(8,128)(2,1)S(1)} %fusion.7, s32[4,64]{1,0:T(4,128)S(1)} %iota_add_fusion), kind=kOutput, calls=%fused_computation.4 | convolution fusion | flops 34603008 | bytes 394240 | tf_op jit(solution)/shard_map/fau,fkub->kab/dot_general | solution.py:60
  39.8 1.2 %fusion.6 = bf16[4,64,256]{2,1,0:T(8,128)(2,1)S(1)} fusion(f32[4,64,256]{2,1,0:T(8,128)S(1)} %fusion.36, s32[4,64]{1,0:T(4,128)S(1)} %iota_add_fusion, bf16[4,1,2,64,64]{4,3,2,1,0:T(8,128)(2,1)S(1)} %reshape.310), kind=kOutput, calls=%fused_computation.12 | convolution fusion | flops 9568256 | bytes 460800 | tf_op jit(solution)/shard_map/fkuv,fav->fkua/dot_general | solution.py:60
  41.0 1.2 %convolution_bitcast_fusion = f32[256,256]{1,0:T(8,128)S(1)} fusion(bf16[4,64,256]{2,1,0:T(8,128)(2,1)S(1)} %fusion.6, s32[4,64]{1,0:T(4,128)S(1)} %iota_add_fusion), kind=kOutput, calls=%fused_computation.2 | convolution fusion | flops 34603008 | bytes 394240 | tf_op jit(solution)/shard_map/fau,fkub->kab/dot_general | solution.py:60
  42.2 1.2 %fusion.2 = f32[1,256,256]{1,2,0:T(8,128)S(1)} fusion(f32[256,256]{1,0:T(8,128)S(1)} %convolution_bitcast_fusion.2, bf16[4,64,256]{2,1,0:T(8,128)(2,1)S(1)} %fusion.6, s32[4,64]{1,0:T(4,128)S(1)} %iota_add_fusion), kind=kOutput, calls=%fused_computation.8 | convolution fusion | flops 34734080 | bytes 656384 | tf_op jit(solution)/shard_map/fau,fkub->kab/dot_general | solution.py:60
  43.4 1.2 %fusion.30 = (bf16[256,256]{0,1:T(8,128)(2,1)S(1)}, bf16[256,256]{0,1:T(8,128)(2,1)S(1)}) fusion(f32[1,2,256,256]{2,3,1,0:T(8,128)S(1)} %broadcast_select_fusion, f32[1,256,256]{1,2,0:T(8,128)S(1)} %fusion.2, f32[256,256]{1,0:T(8,128)S(1)} %convolution_bitcast_fusion, bf16[4,64,256]{2,1,0:T(8,128)(2,1)S(1)} %fusion.7, s32[4,64]{1,0:T(4,128)S(1)} %iota_add_fusion), kind=kOutput, calls=%fused_computation.63 | convolution fusion | flops 35258368 | bytes 1442816 | tf_op jit(solution)/shard_map/fau,fkub->kab/dot_general | solution.py:60
  44.7 0.2 fusion.204
  44.9 0.2 fusion.206
  45.1 0.2 fusion.205
  45.4 0.2 fusion.207
  45.6 1.4 %fusion.38 = f32[4,64,64]{2,1,0:T(8,128)S(1)} fusion(bf16[4,64,256]{2,1,0:T(8,128)(2,1)S(1)} %fusion.31, s32[4,64]{1,0:T(4,128)S(1)} %iota_add_fusion), kind=kOutput, calls=%fused_computation.77 | convolution fusion | flops 9633792 | bytes 197632 | tf_op jit(solution)/shard_map/fkub,fbv->fkuv/dot_general | solution.py:60
  47.0 1.4 %fusion.35 = f32[4,64,64]{2,1,0:T(8,128)S(1)} fusion(bf16[4,64,256]{2,1,0:T(8,128)(2,1)S(1)} %fusion.31, s32[4,64]{1,0:T(4,128)S(1)} %iota_add_fusion), kind=kOutput, calls=%fused_computation.70 | convolution fusion | flops 9437184 | bytes 197632 | tf_op jit(solution)/shard_map/fkub,fbv->fkuv/dot_general | solution.py:60
  48.4 0.1 fusion.32
  48.5 1.2 %fusion.10 = bf16[4,1,1,64,64]{4,3,0,2,1:T(8,128)(2,1)S(1)} fusion(f32[4,64,64]{2,1,0:T(8,128)S(1)} %fusion.38, bf16[4,64,256]{2,1,0:T(8,128)(2,1)S(1)} %fusion.32, s32[4,64]{1,0:T(4,128)S(1)} %iota_add_fusion), kind=kOutput, calls=%fused_computation.20 | convolution fusion | flops 9469952 | bytes 230400 | tf_op jit(solution)/shard_map/fkub,fbv->fkuv/dot_general | solution.py:60
  49.7 1.2 %fusion.11 = bf16[4,1,1,64,64]{4,3,0,2,1:T(8,128)(2,1)S(1)} fusion(f32[4,64,64]{2,1,0:T(8,128)S(1)} %fusion.35, bf16[4,64,256]{2,1,0:T(8,128)(2,1)S(1)} %fusion.32, s32[4,64]{1,0:T(4,128)S(1)} %iota_add_fusion), kind=kOutput, calls=%fused_computation.21 | convolution fusion | flops 9666560 | bytes 230400 | tf_op jit(solution)/shard_map/fkub,fbv->fkuv/dot_general | solution.py:60
  50.9 0.2 reshape.311
  51.1 8.1 %all_to_all.15 = bf16[4,2,4096]{2,1,0:T(2,128)(2,1)S(1)} all-to-all(bf16[4,2,4096]{2,1,0:T(2,128)(2,1)S(1)} %reshape.311), channel_id=1, replica_groups=mesh['facet'=4,'col'=8] {'facet'}, dimensions={0} | all-to-all | bytes 131072 | tf_op jit(solution)/shard_map/all_to_all | solution.py:121
  59.2 0.1 reshape.312
  59.4 0.7 fusion.46
  60.1 0.7 fusion.45
  60.8 0.7 fusion.18
  61.6 0.4 fusion.57
  62.0 0.4 fusion.53
  62.4 0.7 fusion.19
  63.1 0.4 fusion.14
  63.5 0.4 fusion.15
  63.9 0.6 pad_maximum_fusion.2
  64.5 0.0 reduce-scatter.2.cloned.1.call-update
  64.5 28.8 %reduce-scatter.2.cloned.1.call-done = f32[8,2,128]{2,0,1:T(8,128)} async-done(((f32[64,2,128]{2,0,1:T(8,128)}), f32[8,2,128]{2,0,1:T(8,128)}) %reduce-scatter.2.cloned.1.call-update) | async-done | bytes 8208 | tf_op jit(solution)/shard_map/reduce_scatter | solution.py:131
  93.3 0.7 multiply_bitcast_fusion
  94.0 0.6 copy.35
  (12 shorter events, 0.2 us)
Async XLA Ops:
  6.5 7.3 %copy-start = (f32[4,2,256,256]{3,2,1,0:T(8,128)S(1)}, f32[4,2,256,256]{3,2,1,0:T(8,128)}, u32[]{:S(2)}) copy-start(f32[4,2,256,256]{3,2,1,0:T(8,128)} %param.9) | copy-start | bytes 6291460
  6.5 8.3 %copy-start.1 = (s32[1,4]{1,0:T(1,128)S(1)}, s32[1,4]{1,0:T(1,128)}, u32[]{:S(2)}) copy-start(s32[1,4]{1,0:T(1,128)} %param.6) | copy-start | bytes 52
  8.0 10.0 %all-to-all-start = ((bf16[8,8,2,128]{3,1,2,0:T(8,128)(2,1)}), bf16[8,8,2,128]{3,1,2,0:T(8,128)(2,1)S(1)}, u32[]{:S(2)}, u32[]{:S(2)}) async-start(bf16[8,8,2,128]{3,1,2,0:T(8,128)(2,1)} %stack.31), calls=%async_computation | async-start | bytes 65536 | tf_op jit(solution)/shard_map/all_to_all | solution.py:88
  23.6 10.6 %all-to-all-start.1 = ((bf16[4,2,4096]{2,1,0:T(2,128)(2,1)}), bf16[4,2,4096]{2,1,0:T(2,128)(2,1)S(1)}, u32[]{:S(2)}, u32[]{:S(2)}) async-start(bf16[4,2,4096]{2,1,0:T(2,128)(2,1)} %reshape.309), calls=%async_computation.1 | async-start | bytes 131072 | tf_op jit(solution)/shard_map/all_to_all | solution.py:100
  28.5 64.8 %reduce-scatter.2.cloned.1.call-start = ((), (), s32[]{:S(2)}) async-start(), calls=%async_computation.4 | async-start | bytes 73728 | tf_op jit(solution)/shard_map/reduce_scatter | solution.py:131
Sparse Core Ops, SparseCore 0:
  64.7 28.6 reduce-scatter.1
